TPU v7x, 32 devices: a whole 2x2x4 slice. The times are simulated.
32 devices in a mesh: dp: 8 (over y, x, core), tensor: 4 (over z).
Axes of the slice: x: 2, y: 2, z: 4, core: 2. Of those that a mesh axis runs over, the one named last changes fastest.
Arguments:
- tokens: bfloat16 [8192, 1024], P(('dp', 'tensor')), may hold values from -6 to 6
- lengths: int32 [32], replicated, may hold values from 64 to 832, as said below
- seq_order: int32 [32], replicated, may hold values from 0 to 31, as said below
- gain_attn: bfloat16 [1024], P('dp'), may hold values from 0.5 to 1.5
- w_qkv: bfloat16 [3, 1024, 1024], P(None, 'dp', 'tensor'), may hold values from -0.25 to 0.25
- w_attn_out: bfloat16 [1024, 1024], P('tensor', 'dp'), may hold values from -0.375 to 0.375
- gain_mlp: bfloat16 [1024], P('dp'), may hold values from 0.5 to 1.5
- w_in: bfloat16 [1024, 2, 2624], P('dp', None, 'tensor'), may hold values from -0.1875 to 0.1875
- w_mlp_out: bfloat16 [2624, 1024], P('tensor', 'dp'), may hold values from -0.15625 to 0.15625
- cotangent: bfloat16 [8192, 1024], P(('dp', 'tensor')), may hold values from -6 to 6
Outputs:
- output: bfloat16 [8192, 1024], P(('dp', 'tensor'))
- d_tokens: float32 [8192, 1024], P(('dp', 'tensor'))
- d_gain_attn: float32 [1024], P('dp')
- d_w_qkv: float32 [3, 1024, 1024], P(None, 'dp', 'tensor')
- d_w_attn_out: float32 [1024, 1024], P('tensor', 'dp')
- d_gain_mlp: float32 [1024], P('dp')
- d_w_in: float32 [1024, 2, 2624], P('dp', None, 'tensor')
- d_w_mlp_out: float32 [2624, 1024], P('tensor', 'dp')
Inputs may be any that keep to these rules, and one draw needn't show every extreme that they name: For every g the lengths of the sequences seq_order[g * 4] to seq_order[g * 4 + 3] add up to 1024; in every draw some g holds one sequence of the greatest length and 3 of the least. `seq_order`: each sequence number stands once.
All inputs are finite; a program needn't handle non-finite values.
Results may differ from a plain program's by a relative error of at most 0.017.
Values may be sent and summed in bfloat16 or wider, within the bound.
A program may use at most 128 MiB of HBM per device.

v0:
```python
import jax
import jax.numpy as jnp
from jax import lax
from jax.sharding import PartitionSpec as P

HEAD_DIM = 64
SEQ_GRP = 4
rope_base = 160000.0
norm_eps = 1e-05
masked_fill = -1e30


def layer_norm(field_in, norm_gain):
    row_mean = jnp.mean(field_in, axis=-1, keepdims=True)
    centered = field_in - row_mean
    variance = jnp.mean(centered * centered, axis=-1, keepdims=True)
    return centered * lax.rsqrt(variance + norm_eps) * norm_gain


def rotate(field_in, position):
    half_size = field_in.shape[-1] // 2
    index_range = jnp.arange(half_size, dtype=jnp.float32)
    frequency = rope_base ** (-2.0 * index_range / field_in.shape[-1])
    angles = position[:, None] * frequency[None, :]
    cosine = jnp.cos(angles)[:, None, :]
    sine_part = jnp.sin(angles)[:, None, :]
    first_half = field_in[..., :half_size]
    second_half = field_in[..., half_size:]
    return jnp.concatenate(
        [
            first_half * cosine - second_half * sine_part,
            second_half * cosine + first_half * sine_part,
        ],
        axis=-1,
    )


def geglu(act_part, up_part):
    return jax.nn.gelu(act_part, approximate=False) * up_part


def layout(lengths, seq_order, group_rows):
    seq_total = seq_order.shape[0]
    first_seq = lax.axis_index("dp") * SEQ_GRP
    chosen = lax.dynamic_slice_in_dim(seq_order, first_seq, SEQ_GRP)
    matched = chosen[:, None] == jnp.arange(seq_total, dtype=jnp.int32)[None, :]
    dealt_lengths = jnp.sum(jnp.where(matched, lengths[None, :], 0), axis=1)
    seq_ends = jnp.cumsum(dealt_lengths)
    row_index = jnp.arange(group_rows, dtype=jnp.int32)
    passed = row_index[:, None] >= seq_ends[None, :]
    segment = jnp.sum(passed.astype(jnp.int32), axis=1)
    row_start = jnp.sum(jnp.where(passed, dealt_lengths[None, :], 0), axis=1)
    return (segment, (row_index - row_start).astype(jnp.float32))


def item_layout(array_in, block_rows):
    group_rows, head_count, head_size = array_in.shape
    block_count = group_rows // block_rows
    shaped = array_in.reshape(block_count, block_rows, head_count, head_size)
    return shaped.transpose(2, 0, 1, 3).reshape(head_count * block_count, block_rows, head_size)


def from_items(items, group_rows):
    item_count, block_rows, head_size = items.shape
    block_count = group_rows // block_rows
    head_count = item_count // block_count
    shaped = items.reshape(head_count, block_count, block_rows, head_size)
    return shaped.transpose(1, 2, 0, 3).reshape(group_rows, head_count, head_size)


def masked_scores(query_block, key_head, segment_block, segment):
    score_scale = query_block.shape[-1] ** (-0.5)
    raw_scores = lax.dot_general(
        query_block, key_head, (((1,), (1,)), ((), ())), preferred_element_type=jnp.float32
    )
    allowed = segment_block[:, None] == segment[None, :]
    return jnp.where(allowed, raw_scores * score_scale, masked_fill)


def attend_forward(query_rot, key_rot, value_low, segment, block_rows):
    group_rows, head_count, head_size = query_rot.shape
    block_count = group_rows // block_rows
    query_items = item_layout(query_rot, block_rows)
    key_heads = key_rot.transpose(1, 0, 2)
    value_heads = value_low.transpose(1, 0, 2)
    segment_blocks = segment.reshape(block_count, block_rows)

    def one_item(item_index):
        head_index = item_index // block_count
        block_index = item_index % block_count
        query_block = lax.dynamic_index_in_dim(query_items, item_index, 0, False)
        key_head = lax.dynamic_index_in_dim(key_heads, head_index, 0, False)
        value_head = lax.dynamic_index_in_dim(value_heads, head_index, 0, False)
        segment_block = lax.dynamic_index_in_dim(segment_blocks, block_index, 0, False)
        scores = masked_scores(query_block, key_head, segment_block, segment)
        row_top = jnp.max(scores, axis=1, keepdims=True)
        weights = jnp.exp(scores - row_top)
        row_total = jnp.sum(weights, axis=1, keepdims=True)
        probs_low = (weights / row_total).astype(jnp.bfloat16)
        result = jnp.dot(probs_low, value_head, preferred_element_type=jnp.float32)
        return (result, row_top[:, 0] + jnp.log(row_total[:, 0]))

    results, log_totals = lax.map(one_item, jnp.arange(head_count * block_count, dtype=jnp.int32))
    return (from_items(results, group_rows), log_totals)


def attend_backward(query_rot, key_rot, value_low, grad_out, log_totals, segment, block_rows):
    group_rows, head_count, head_size = query_rot.shape
    block_count = group_rows // block_rows
    score_scale = head_size ** (-0.5)
    query_items = item_layout(query_rot, block_rows)
    grad_items = item_layout(grad_out, block_rows)
    key_heads = key_rot.transpose(1, 0, 2)
    value_heads = value_low.transpose(1, 0, 2)
    segment_blocks = segment.reshape(block_count, block_rows)

    def one_item(carried, item_index):
        key_grads, value_grads = carried
        head_index = item_index // block_count
        block_index = item_index % block_count
        query_block = lax.dynamic_index_in_dim(query_items, item_index, 0, False)
        grad_block = lax.dynamic_index_in_dim(grad_items, item_index, 0, False)
        log_row = lax.dynamic_index_in_dim(log_totals, item_index, 0, False)
        key_head = lax.dynamic_index_in_dim(key_heads, head_index, 0, False)
        value_head = lax.dynamic_index_in_dim(value_heads, head_index, 0, False)
        segment_block = lax.dynamic_index_in_dim(segment_blocks, block_index, 0, False)
        scores = masked_scores(query_block, key_head, segment_block, segment)
        prob_full = jnp.exp(scores - log_row[:, None])
        probs_low = prob_full.astype(jnp.bfloat16)
        grad_probs = lax.dot_general(
            grad_block, value_head, (((1,), (1,)), ((), ())), preferred_element_type=jnp.float32
        )
        row_delta = jnp.sum(prob_full * grad_probs, axis=1, keepdims=True)
        grad_scores = (prob_full * (grad_probs - row_delta)).astype(jnp.bfloat16)
        grad_query = (
            jnp.dot(grad_scores, key_head, preferred_element_type=jnp.float32) * score_scale
        )
        grad_key = (
            lax.dot_general(
                grad_scores,
                query_block,
                (((0,), (0,)), ((), ())),
                preferred_element_type=jnp.float32,
            )
            * score_scale
        )
        grad_value = lax.dot_general(
            probs_low, grad_block, (((0,), (0,)), ((), ())), preferred_element_type=jnp.float32
        )
        key_grads = lax.dynamic_update_index_in_dim(
            key_grads,
            lax.dynamic_index_in_dim(key_grads, head_index, 0, False) + grad_key,
            head_index,
            0,
        )
        value_grads = lax.dynamic_update_index_in_dim(
            value_grads,
            lax.dynamic_index_in_dim(value_grads, head_index, 0, False) + grad_value,
            head_index,
            0,
        )
        return ((key_grads, value_grads), grad_query)

    zero_heads = jnp.zeros((head_count, group_rows, head_size), jnp.float32)
    (key_grads, value_grads), query_grads = lax.scan(
        one_item, (zero_heads, zero_heads), jnp.arange(head_count * block_count, dtype=jnp.int32)
    )
    return (
        from_items(query_grads, group_rows),
        key_grads.transpose(1, 0, 2),
        value_grads.transpose(1, 0, 2),
    )


def spread_rows(local_rows):
    return lax.all_gather(local_rows, "tensor", axis=0, tiled=True)


def spread_grads(local_grads):
    return lax.all_gather(local_grads, "tensor", axis=0, tiled=True)


def sum_heads(activations, weight_part, row_count):

    def row_term(first_row, row_number):
        return jnp.dot(activations, weight_part, preferred_element_type=jnp.float32)

    return lax.psum_scatter(
        row_term(jnp.int32(0), row_count * lax.axis_size("tensor")),
        "tensor",
        scatter_dimension=0,
        tiled=True,
    )


def sum_grads(grads_low, weight_full, einsum_form, row_count):

    def row_term(first_row, row_number):
        return jnp.einsum(einsum_form, grads_low, weight_full, preferred_element_type=jnp.float32)

    return lax.psum_scatter(
        row_term(jnp.int32(0), row_count * lax.axis_size("tensor")),
        "tensor",
        scatter_dimension=0,
        tiled=True,
    )


def local(
    tokens, lengths, seq_order, gain_attn, w_qkv, w_attn_out, gain_mlp, w_in, w_mlp_out, cotangent
):
    row_count = tokens.shape[0]
    group_rows = row_count * lax.axis_size("tensor")
    block_rows = min(512, group_rows)
    segment, position = layout(lengths, seq_order, group_rows)
    gain_low_one, qkv_weight, out_weight, gain_low_two, in_weight, down_weight = (
        lax.all_gather(gain_attn, "dp", axis=0, tiled=True),
        lax.all_gather(w_qkv, "dp", axis=1, tiled=True),
        lax.all_gather(w_attn_out, "dp", axis=1, tiled=True),
        lax.all_gather(gain_mlp, "dp", axis=0, tiled=True),
        lax.all_gather(w_in, "dp", axis=0, tiled=True),
        lax.all_gather(w_mlp_out, "dp", axis=1, tiled=True),
    )
    gain_one = gain_low_one.astype(jnp.float32)
    gain_two = gain_low_two.astype(jnp.float32)
    residual = tokens.astype(jnp.float32)
    normed_one = spread_rows(layer_norm(residual, gain_one).astype(jnp.bfloat16))
    qkv = jnp.einsum("rd,pdc->rpc", normed_one, qkv_weight, preferred_element_type=jnp.float32)
    head_count = qkv.shape[2] // HEAD_DIM
    head_shape = (group_rows, head_count, HEAD_DIM)
    query_rot = rotate(qkv[:, 0].reshape(head_shape), position).astype(jnp.bfloat16)
    key_rot = rotate(qkv[:, 1].reshape(head_shape), position).astype(jnp.bfloat16)
    value_low = qkv[:, 2].reshape(head_shape).astype(jnp.bfloat16)
    attended, log_totals = attend_forward(query_rot, key_rot, value_low, segment, block_rows)
    attn_low = attended.reshape(group_rows, head_count * HEAD_DIM).astype(jnp.bfloat16)
    resid_mid = residual + sum_heads(attn_low, out_weight, row_count)
    normed_two = spread_rows(layer_norm(resid_mid, gain_two).astype(jnp.bfloat16))
    gate_up = jnp.einsum("rd,dpc->rpc", normed_two, in_weight, preferred_element_type=jnp.float32)
    hidden = geglu(gate_up[:, 0], gate_up[:, 1]).astype(jnp.bfloat16)
    output = (resid_mid + sum_heads(hidden, down_weight, row_count)).astype(jnp.bfloat16)
    grad_two = spread_grads(cotangent)
    d_hidden = lax.dot_general(
        grad_two, down_weight, (((1,), (1,)), ((), ())), preferred_element_type=jnp.float32
    )
    d_down = lax.dot_general(
        hidden, grad_two, (((0,), (0,)), ((), ())), preferred_element_type=jnp.float32
    )
    geglu_pull = jax.vjp(geglu, gate_up[:, 0], gate_up[:, 1])[1]
    d_act, d_up = geglu_pull(d_hidden)
    d_gate_up = jnp.stack([d_act, d_up], axis=1).astype(jnp.bfloat16)
    d_in = jnp.einsum("rd,rpc->dpc", normed_two, d_gate_up, preferred_element_type=jnp.float32)
    d_normed_two = sum_grads(d_gate_up, in_weight, "rpc,dpc->rd", row_count)
    norm_pull_two = jax.vjp(layer_norm, resid_mid, gain_two)[1]
    d_mid_norm, d_gain_two = norm_pull_two(d_normed_two)
    d_mid = cotangent.astype(jnp.float32) + d_mid_norm
    grad_one = spread_grads(d_mid.astype(jnp.bfloat16))
    d_out = lax.dot_general(
        attn_low, grad_one, (((0,), (0,)), ((), ())), preferred_element_type=jnp.float32
    )
    d_att = lax.dot_general(
        grad_one, out_weight, (((1,), (1,)), ((), ())), preferred_element_type=jnp.float32
    ).astype(jnp.bfloat16)
    d_query_rot, d_key_rot, d_value = attend_backward(
        query_rot, key_rot, value_low, d_att.reshape(head_shape), log_totals, segment, block_rows
    )
    rotate_pull = jax.vjp(lambda field_in: rotate(field_in, position), d_query_rot)[1]
    d_query = rotate_pull(d_query_rot)[0]
    d_key = rotate_pull(d_key_rot)[0]
    flat_shape = (group_rows, head_count * HEAD_DIM)
    d_qkv = jnp.stack(
        [d_query.reshape(flat_shape), d_key.reshape(flat_shape), d_value.reshape(flat_shape)],
        axis=1,
    ).astype(jnp.bfloat16)
    d_qkv_weight = jnp.einsum("rd,rpc->pdc", normed_one, d_qkv, preferred_element_type=jnp.float32)
    d_normed_one = sum_grads(d_qkv, qkv_weight, "rpc,pdc->rd", row_count)
    norm_pull_one = jax.vjp(layer_norm, residual, gain_one)[1]
    d_first, d_gain_one = norm_pull_one(d_normed_one)
    d_tokens = d_mid + d_first
    gain_sums = lax.psum((d_gain_one, d_gain_two), "tensor")
    shares = (
        lax.psum_scatter(gain_sums[0], "dp", scatter_dimension=0, tiled=True),
        lax.psum_scatter(d_qkv_weight, "dp", scatter_dimension=1, tiled=True),
        lax.psum_scatter(d_out, "dp", scatter_dimension=1, tiled=True),
        lax.psum_scatter(gain_sums[1], "dp", scatter_dimension=0, tiled=True),
        lax.psum_scatter(d_in, "dp", scatter_dimension=0, tiled=True),
        lax.psum_scatter(d_down, "dp", scatter_dimension=1, tiled=True),
    )
    return (output, d_tokens, shares[0], shares[1], shares[2], shares[3], shares[4], shares[5])


def solution(mesh):
    return jax.shard_map(
        local,
        mesh=mesh,
        in_specs=(
            P(("dp", "tensor"), None),
            P(),
            P(),
            P("dp"),
            P(None, "dp", "tensor"),
            P("tensor", "dp"),
            P("dp"),
            P("dp", None, "tensor"),
            P("tensor", "dp"),
            P(("dp", "tensor"), None),
        ),
        out_specs=(
            P(("dp", "tensor"), None),
            P(("dp", "tensor"), None),
            P("dp"),
            P(None, "dp", "tensor"),
            P("tensor", "dp"),
            P("dp"),
            P("dp", None, "tensor"),
            P("tensor", "dp"),
        ),
        check_vma=False,
    )
```

profile of v0, /device:TPU:0, one launch (start us, length us, event | category | flops | bytes accessed | tf_op | source)
XLA Modules:
  0.0 1052.6 jit_solution(94516916821931615)
XLA Ops:
  9.1 10.3 all-gather
  21.9 2.1 fusion.77
  24.8 12.0 %all_gather.33 = bf16[256,1024]{1,0:T(8,128)(2,1)} all-gather(bf16[256,128]{1,0:T(8,128)(2,1)S(1)} %copy-done.20), channel_id=1, replica_groups=mesh['dp'=8,'tensor'=4] {'dp'}, dimensions={1}, use_global_device_ids=true | all-gather | bytes 589824 | tf_op jit(solution)/shard_map/all_gather | solution.py:219
  39.8 48.1 %all-gather.10.cloned.1.call-done = bf16[1024,1024]{1,0:T(8,128)(2,1)} async-done(((bf16[256,1024]{1,0:T(8,128)(2,1)}), bf16[1024,1024]{1,0:T(8,128)(2,1)}) %all-gather.10.cloned.1.call-update) | async-done | bytes 2097168 | tf_op jit(solution)/shard_map/all_gather | solution.py:176
  87.9 3.9 fusion.64
  96.9 70.2 %while.32 = (s32[]{:T(128)}, bf16[8,512,64]{1,2,0:T(8,128)(2,1)}, f32[8,512]{1,0:T(8,128)S(1)}, s32[8]{0:T(128)S(1)}, s32[2,512]{1,0:T(2,128)S(1)}, /*index=5*/s...) while((s32[]{:T(128)}, bf16[8,512,64]{1,2,0:T(8,128)(2,1)}, ...), condition=%wide.region_9.10_spmd.clone, body=%wide.region_6.9_spmd.sunk.clone | while | flops 138935840 | bytes 7109525 | solution.py:103
  103.4 2.2 fusion.152
  112.2 2.2 fusion.152
  121.0 2.2 fusion.152
  129.8 2.2 fusion.152
  138.5 2.2 fusion.152
  147.3 2.2 fusion.152
  156.1 2.2 fusion.152
  164.8 2.2 fusion.152
  169.0 3.7 fusion.94
  174.6 8.7 all-gather.1
  183.3 65.1 %reduce-scatter.9.cloned.1.call-done = f32[256,1024]{1,0:T(8,128)} async-done(((f32[1024,1024]{1,0:T(8,128)}), f32[256,1024]{1,0:T(8,128)}) %reduce-scatter.9.cloned.1.call-update) | async-done | bytes 1048592 | tf_op jit(solution)/shard_map/reduce_scatter | solution.py:188
  251.7 24.1 %all-gather.18.cloned.1.call-done = bf16[656,1024]{1,0:T(8,128)(2,1)} async-done(((bf16[656,128]{1,0:T(8,128)(2,1)}), bf16[656,1024]{1,0:T(8,128)(2,1)}) %all-gather.18.cloned.1.call-update) | async-done | bytes 1343504 | tf_op jit(solution)/shard_map/all_gather | solution.py:222
  275.7 47.5 %all-gather.20.cloned.1.call-done = bf16[1024,1024]{1,0:T(8,128)(2,1)} async-done(((bf16[256,1024]{1,0:T(8,128)(2,1)}), bf16[1024,1024]{1,0:T(8,128)(2,1)}) %all-gather.20.cloned.1.call-update) | async-done | bytes 2097168 | tf_op jit(solution)/shard_map/all_gather | solution.py:180
  323.2 5.1 fusion.96
  328.3 26.4 %all-gather.16.cloned.1.call-done = bf16[1024,2,656]{0,2,1:T(8,128)(2,1)} async-done(((bf16[128,2,656]{0,2,1:T(8,128)(2,1)}), bf16[1024,2,656]{0,2,1:T(8,128)(2,1)}) %all-gather.16.cloned.1.call-update) | async-done | bytes 2686992 | tf_op jit(solution)/shard_map/all_gather | solution.py:221
  354.6 48.2 %all-gather.14.cloned.1.call-done = bf16[1024,1024]{1,0:T(8,128)(2,1)} async-done(((bf16[256,1024]{1,0:T(8,128)(2,1)}), bf16[1024,1024]{1,0:T(8,128)(2,1)}) %all-gather.14.cloned.1.call-update) | async-done | bytes 2097168 | tf_op jit(solution)/shard_map/all_gather | solution.py:176
  402.8 5.5 fusion.60
  408.4 6.5 fusion.74
  417.4 5.0 convolution_bitcast_fusion.2
  422.5 5.3 fusion.95
  427.8 70.2 %reduce-scatter.13.cloned.1.call-done = f32[256,1024]{1,0:T(8,128)} async-done(((f32[1024,1024]{1,0:T(8,128)}), f32[256,1024]{1,0:T(8,128)}) %reduce-scatter.13.cloned.1.call-update) | async-done | bytes 1048592 | tf_op jit(solution)/shard_map/reduce_scatter | solution.py:201
  499.6 78.0 %reduce-scatter.11.cloned.1.call-done = f32[256,1024]{1,0:T(8,128)} async-done(((f32[1024,1024]{1,0:T(8,128)}), f32[256,1024]{1,0:T(8,128)}) %reduce-scatter.11.cloned.1.call-update) | async-done | bytes 1048592 | tf_op jit(solution)/shard_map/reduce_scatter | solution.py:188
  577.6 2.7 fusion.89
  582.6 46.4 %all-gather.22.cloned.1.call-done = bf16[1024,1024]{1,0:T(8,128)(2,1)} async-done(((bf16[256,1024]{1,0:T(8,128)(2,1)}), bf16[1024,1024]{1,0:T(8,128)(2,1)}) %all-gather.22.cloned.1.call-update) | async-done | bytes 2097168 | tf_op jit(solution)/shard_map/all_gather | solution.py:180
  628.9 2.3 convolution_convert_fusion
  635.4 122.5 %while.33 = (s32[]{:T(128)}, f32[4,1024,64]{1,2,0:T(8,128)}, f32[4,1024,64]{1,2,0:T(8,128)}, f32[8,512,64]{1,2,0:T(8,128)}, s32[8]{0:T(128)S(1)}, /*index=5*/s32...) while((s32[]{:T(128)}, f32[4,1024,64]{1,2,0:T(8,128)}, ...), condition=%wide.region_19.20_spmd.clone, body=%wide.region_17.19_spmd.sunk.clone | while | flops 341016096 | bytes 19289032 | solution.py:165
  662.1 2.1 fusion.164
  738.6 2.1 fusion.164
  753.9 2.1 fusion.164
  757.9 3.1 copy.98
  761.0 2.1 reshape.229
  765.6 5.1 fusion.66
  770.8 5.2 convolution_bitcast_fusion.1
  777.5 4.8 fusion.98
  783.6 7.2 fusion.58
  795.6 20.2 %reduce-scatter.17.cloned.1.call-done = f32[3,128,256]{1,2,0:T(8,128)} async-done(((f32[3,1024,256]{1,2,0:T(8,128)}), f32[3,128,256]{1,2,0:T(8,128)}) %reduce-scatter.17.cloned.1.call-update) | async-done | bytes 393232 | tf_op jit(solution)/shard_map/reduce_scatter | solution.py:282
  817.7 77.0 %reduce-scatter.15.cloned.1.call-done = f32[256,1024]{1,0:T(8,128)} async-done(((f32[1024,1024]{1,0:T(8,128)}), f32[256,1024]{1,0:T(8,128)}) %reduce-scatter.15.cloned.1.call-update) | async-done | bytes 1048592 | tf_op jit(solution)/shard_map/reduce_scatter | solution.py:201
  898.2 14.0 %all-reduce.6 = (f32[1024]{0:T(1024)S(1)}, f32[1024]{0:T(1024)S(1)}) all-reduce(f32[1024]{0:T(1024)S(1)} %get-tuple-element.431, f32[1024]{0:T(1024)S(1)} %get-tuple-element.429), channel_id=6, replica_groups=mesh['dp'=8,'tensor'=4] {'dp'}, use_global_device_ids=true, to_apply=%region_25.26.clone | all-reduce | flops 2048 | bytes 16384
  912.3 11.6 %all-reduce.7 = (f32[128]{0:T(128)}, f32[128]{0:T(128)}) all-reduce(f32[128]{0:T(128)S(1)} %dynamic-slice.1, f32[128]{0:T(128)S(1)} %dynamic-slice.3), channel_id=1, replica_groups=mesh['dp'=8,'tensor'=4] {'tensor'}, use_global_device_ids=true, to_apply=%region_24.25 | all-reduce | flops 256 | bytes 2048 | tf_op jit(solution)/shard_map/psum | solution.py:279
  925.4 19.0 %reduce-scatter.23.cloned.1.call-done = f32[656,128]{1,0:T(8,128)} async-done(((f32[656,1024]{1,0:T(8,128)}), f32[656,128]{1,0:T(8,128)}) %reduce-scatter.23.cloned.1.call-update) | async-done | bytes 335888 | tf_op jit(solution)/shard_map/reduce_scatter | solution.py:286
  944.4 61.5 %reduce-scatter.21.cloned.1.call-done = f32[128,2,656]{0,2,1:T(8,128)} async-done(((f32[1024,2,656]{0,2,1:T(8,128)}), f32[128,2,656]{0,2,1:T(8,128)}) %reduce-scatter.21.cloned.1.call-update) | async-done | bytes 671760 | tf_op jit(solution)/shard_map/reduce_scatter | solution.py:285
  1005.9 40.0 %reduce-scatter.19.cloned.1.call-done = f32[256,128]{1,0:T(8,128)} async-done(((f32[256,1024]{1,0:T(8,128)}), f32[256,128]{1,0:T(8,128)}) %reduce-scatter.19.cloned.1.call-update) | async-done | bytes 131088 | tf_op jit(solution)/shard_map/reduce_scatter | solution.py:283
  (271 shorter events, 152.6 us)
Async XLA Ops:
  7.2 17.0 %copy-start.23 = (s32[32]{0:T(128)S(1)}, s32[32]{0:T(128)}, u32[]{:S(2)}) copy-start(s32[32]{0:T(128)} %param.16) | copy-start | bytes 388
  7.2 17.1 %copy-start.24 = (s32[32]{0:T(128)S(1)}, s32[32]{0:T(128)}, u32[]{:S(2)}) copy-start(s32[32]{0:T(128)} %param.15) | copy-start | bytes 388
  7.2 17.6 %copy-start.20 = (bf16[256,128]{1,0:T(8,128)(2,1)S(1)}, bf16[256,128]{1,0:T(8,128)(2,1)}, u32[]{:S(2)}) copy-start(bf16[256,128]{1,0:T(8,128)(2,1)} %param.19) | copy-start | bytes 196612
  7.2 32.6 %all-gather.12.cloned.1.call-start = ((), (), s32[]{:S(2)}) async-start(), calls=%async_computation.9 | async-start | bytes 1769472 | tf_op jit(solution)/shard_map/all_gather | solution.py:218
  9.0 78.9 %all-gather.10.cloned.1.call-start = ((), (), s32[]{:S(2)}) async-start(), calls=%async_computation.8 | async-start | bytes 2621440 | tf_op jit(solution)/shard_map/all_gather | solution.py:176
  24.1 224.3 %reduce-scatter.9.cloned.1.call-start = ((), (), s32[]{:S(2)}) async-start(), calls=%async_computation.10 | async-start | bytes 5242880 | tf_op jit(solution)/shard_map/reduce_scatter | solution.py:188
  38.2 53.9 %copy-start.16 = (f32[1024,32]{0,1:T(8,128)}, f32[1024,32]{0,1:T(8,128)S(1)}, u32[]{:S(2)}) copy-start(f32[1024,32]{0,1:T(8,128)S(1)} %get-tuple-element.510) | copy-start | bytes 393220
  38.2 53.9 %copy-start.18 = (f32[1024,32]{0,1:T(8,128)}, f32[1024,32]{0,1:T(8,128)S(1)}, u32[]{:S(2)}) copy-start(f32[1024,32]{0,1:T(8,128)S(1)} %get-tuple-element.511) | copy-start | bytes 393220
  167.0 1.9 copy-start.6
  172.8 1.8 copy-start.21
  172.8 75.7 %copy-start = (bf16[256,1024]{1,0:T(8,128)(2,1)S(1)}, bf16[256,1024]{1,0:T(8,128)(2,1)}, u32[]{:S(2)}) copy-start(bf16[256,1024]{1,0:T(8,128)(2,1)} %param.14) | copy-start | bytes 1572868
  172.8 102.9 %all-gather.18.cloned.1.call-start = ((), (), s32[]{:S(2)}) async-start(), calls=%async_computation.13 | async-start | bytes 1511424 | tf_op jit(solution)/shard_map/all_gather | solution.py:222
  173.4 149.8 %all-gather.20.cloned.1.call-start = ((), (), s32[]{:S(2)}) async-start(), calls=%async_computation.15 | async-start | bytes 2621440 | tf_op jit(solution)/shard_map/all_gather | solution.py:180
  174.0 180.7 %all-gather.16.cloned.1.call-start = ((), (), s32[]{:S(2)}) async-start(), calls=%async_computation.12 | async-start | bytes 3022848 | tf_op jit(solution)/shard_map/all_gather | solution.py:221
  174.6 228.3 %all-gather.14.cloned.1.call-start = ((), (), s32[]{:S(2)}) async-start(), calls=%async_computation.11 | async-start | bytes 2621440 | tf_op jit(solution)/shard_map/all_gather | solution.py:176
  251.2 246.9 %reduce-scatter.13.cloned.1.call-start = ((), (), s32[]{:S(2)}) async-start(), calls=%async_computation.16 | async-start | bytes 5242880 | tf_op jit(solution)/shard_map/reduce_scatter | solution.py:201
  402.8 5.5 copy-start.2
  414.8 1.6 copy-start.11
  414.8 2.6 copy-start.22
  416.3 1.1 copy-start.13
  416.4 6.1 copy-start.14
  422.4 155.2 %reduce-scatter.11.cloned.1.call-start = ((), (), s32[]{:S(2)}) async-start(), calls=%async_computation.14 | async-start | bytes 5242880 | tf_op jit(solution)/shard_map/reduce_scatter | solution.py:188
  427.8 201.2 %all-gather.22.cloned.1.call-start = ((), (), s32[]{:S(2)}) async-start(), calls=%async_computation.17 | async-start | bytes 2621440 | tf_op jit(solution)/shard_map/all_gather | solution.py:180
  499.6 81.7 %copy-start.7 = (bf16[256,1024]{1,0:T(8,128)(2,1)S(1)}, bf16[256,1024]{1,0:T(8,128)(2,1)}, u32[]{:S(2)}) copy-start(bf16[256,1024]{1,0:T(8,128)(2,1)} %param.23) | copy-start | bytes 1572868
  499.6 129.3 %copy-start.10 = (bf16[256,1024]{1,0:T(8,128)(2,1)S(1)}, bf16[256,1024]{1,0:T(8,128)(2,1)}, u32[]{:S(2)}) copy-start(bf16[256,1024]{1,0:T(8,128)(2,1)} %all_gather.33) | copy-start | bytes 1572868
  580.3 1.0 copy-start.4
  582.3 233.5 %reduce-scatter.17.cloned.1.call-start = ((), (), s32[]{:S(2)}) async-start(), calls=%async_computation.19 | async-start | bytes 3538944 | tf_op jit(solution)/shard_map/reduce_scatter | solution.py:282
  757.9 5.2 copy-start.1
  757.9 5.2 copy-start.17
  757.9 5.3 copy-start.19
  770.7 124.1 %reduce-scatter.15.cloned.1.call-start = ((), (), s32[]{:S(2)}) async-start(), calls=%async_computation.18 | async-start | bytes 5242880 | tf_op jit(solution)/shard_map/reduce_scatter | solution.py:201
  776.0 1.5 copy-start.15
  776.0 168.4 %reduce-scatter.23.cloned.1.call-start = ((), (), s32[]{:S(2)}) async-start(), calls=%async_computation.22 | async-start | bytes 3022848 | tf_op jit(solution)/shard_map/reduce_scatter | solution.py:286
  782.3 1.4 copy-start.12
  782.3 223.6 %reduce-scatter.21.cloned.1.call-start = ((), (), s32[]{:S(2)}) async-start(), calls=%async_computation.21 | async-start | bytes 6045696 | tf_op jit(solution)/shard_map/reduce_scatter | solution.py:285
  790.9 1.8 copy-start.9
  790.9 3.5 copy-start.25
  790.9 255.0 %reduce-scatter.19.cloned.1.call-start = ((), (), s32[]{:S(2)}) async-start(), calls=%async_computation.20 | async-start | bytes 1179648 | tf_op jit(solution)/shard_map/reduce_scatter | solution.py:283
  794.4 129.6 %copy-start.5 = (f32[256,1024]{1,0:T(8,128)S(1)}, f32[256,1024]{1,0:T(8,128)}, u32[]{:S(2)}) copy-start(f32[256,1024]{1,0:T(8,128)} %copy-done.4) | copy-start | bytes 3145732
  794.4 129.6 %copy-start.8 = (bf16[256,1024]{1,0:T(8,128)(2,1)S(1)}, bf16[256,1024]{1,0:T(8,128)(2,1)}, u32[]{:S(2)}) copy-start(bf16[256,1024]{1,0:T(8,128)(2,1)} %param.23) | copy-start | bytes 1572868
  894.8 29.2 %copy-start.3 = (f32[256,1024]{1,0:T(8,128)S(1)}, f32[256,1024]{1,0:T(8,128)}, u32[]{:S(2)}) copy-start(f32[256,1024]{1,0:T(8,128)} %reduce-scatter.15.cloned.1.call-done) | copy-start | bytes 3145732
Sparse Core Ops, SparseCore 0:
  10.5 29.2 all-gather.11
  42.0 45.9 all-gather.9
  172.9 75.4 reduce-scatter.8
  250.3 25.3 all-gather.17
  277.2 45.9 all-gather.19
  325.1 29.4 all-gather.15
  356.9 45.9 all-gather.13
  422.5 75.4 reduce-scatter.12
  500.3 77.2 reduce-scatter.10
  582.5 46.4 all-gather.21
  770.8 44.9 reduce-scatter.16
  818.0 76.7 reduce-scatter.14
  899.2 45.1 reduce-scatter.22
  948.6 57.1 reduce-scatter.20
  1009.8 36.0 reduce-scatter.18
where the time goes:
time: 1060 us; the launch traced here: 1050 us
  waiting for transfers between devices  675 us (64%)
  matrix products  159 us (15%)
  loops' own time  63.2 us (6%)
  blocking collectives  56.7 us (5%)
  local copies, waits for them, and re-layouts  45.3 us (4%)
  other arithmetic  37.3 us (4%)
  between operations  15.3 us (1%)
    reduce_scatter x2, waiting for transfers between devices, sum_grads(): lax.psum_scatter(row_term(jnp.int32(0), row_count * lax.axis_size('tensor...  147 us
    reduce_scatter x2, waiting for transfers between devices, sum_heads(): lax.psum_scatter(row_term(jnp.int32(0), row_count * lax.axis_size('tensor...  143 us
    all_gather x2, waiting for transfers between devices, spread_rows(): return lax.all_gather(local_rows, 'tensor', axis=0, tiled=True)  96.3 us
    all_gather x2, waiting for transfers between devices, spread_grads(): return lax.all_gather(local_grads, 'tensor', axis=0, tiled=True)  93.8 us
    reduce_scatter x1, waiting for transfers between devices, local(): lax.psum_scatter(d_in, 'dp', scatter_dimension=0, tiled=True)  61.5 us
    reduce_scatter x1, waiting for transfers between devices, local(): lax.psum_scatter(d_out, 'dp', scatter_dimension=1, tiled=True)  40 us
    another operation x1, loops' own time, attend_backward(): lax.scan(one_item, (zero_heads, zero_heads), jnp.arange(head_count * bloc...  31.6 us
    another operation x1, loops' own time, attend_forward(): lax.map(one_item, jnp.arange(head_count * block_count, dtype=jnp.int32))  31.5 us
  transfers between devices with their start and end apart: 15, of which 15 were waited for; matrix products, arithmetic and copies ran while one was open for 5% of the time, Pallas kernels for 0%

commit v1 on v0

--- a/solution.py
+++ b/solution.py
@@ -8,6 +8,19 @@
 rope_base = 160000.0
 norm_eps = 1e-05
 masked_fill = -1e30
+
+
+def collect(value, axis, dim):
+    count, mine, rows = (lax.axis_size(axis), lax.axis_index(axis), value.shape[dim])
+    right = [(i, (i + 1) % count) for i in range(count)]
+    out = jnp.zeros((*value.shape[:dim], count * rows, *value.shape[dim + 1 :]), value.dtype)
+    held = value
+    for step in range(count):
+        source = (mine - step) % count
+        out = lax.dynamic_update_slice_in_dim(out, held, source * rows, axis=dim)
+        if step < count - 1:
+            held = lax.ppermute(held, axis, right)
+    return out
 
 
 def layer_norm(field_in, norm_gain):
@@ -177,7 +190,7 @@
 
 
 def spread_grads(local_grads):
-    return lax.all_gather(local_grads, "tensor", axis=0, tiled=True)
+    return collect(local_grads, "tensor", 0)
 
 
 def sum_heads(activations, weight_part, row_count):

time: 1060 us -> 1020 us (0.962)
  waiting for transfers between devices: 675 us -> 614 us
  local copies, waits for them, and re-layouts: 45.3 us -> 59.2 us
    all_gather x2 -> x0, waiting for transfers between devices: 93.8 us -> none  [spread_grads(): return lax.all_gather(local_grads, 'tensor', axis=0, tiled=True)]
    ppermute x0 -> x6, waiting for transfers between devices: none -> 78 us  [collect(): held = lax.ppermute(held, axis, right)]
    all_gather x1, waiting for transfers between devices: 24.1 us -> 0.01 us  [local(): lax.all_gather(w_mlp_out, 'dp', axis=1, tiled=True)]
    all_gather x1, waiting for transfers between devices: 26.4 us -> 5.52 us  [local(): lax.all_gather(w_in, 'dp', axis=0, tiled=True)]
  transfers between devices with their start and end apart: 15 -> 19, of which waited for: 15 -> 18; matrix products, arithmetic and copies ran while one was open for 5% -> 6% of each run, Pallas kernels for 0% -> 0%
where the time goes in v1:
time: 1020 us; the launch traced here: 1010 us
  waiting for transfers between devices  614 us (60%)
  matrix products  158 us (15%)
  loops' own time  63.2 us (6%)
  local copies, waits for them, and re-layouts  59.2 us (6%)
  blocking collectives  56.6 us (6%)
  other arithmetic  36.3 us (4%)
  between operations  15.4 us (2%)
    reduce_scatter x2, waiting for transfers between devices, sum_grads(): lax.psum_scatter(row_term(jnp.int32(0), row_count * lax.axis_size('tensor...  147 us
    reduce_scatter x2, waiting for transfers between devices, sum_heads(): lax.psum_scatter(row_term(jnp.int32(0), row_count * lax.axis_size('tensor...  144 us
    all_gather x2, waiting for transfers between devices, spread_rows(): return lax.all_gather(local_rows, 'tensor', axis=0, tiled=True)  96.1 us
    ppermute x6, waiting for transfers between devices, collect(): held = lax.ppermute(held, axis, right)  78 us
    reduce_scatter x1, waiting for transfers between devices, local(): lax.psum_scatter(d_in, 'dp', scatter_dimension=0, tiled=True)  61.5 us
    reduce_scatter x1, waiting for transfers between devices, local(): lax.psum_scatter(d_out, 'dp', scatter_dimension=1, tiled=True)  40.2 us
    another operation x1, loops' own time, attend_backward(): lax.scan(one_item, (zero_heads, zero_heads), jnp.arange(head_count * bloc...  31.6 us
    another operation x1, loops' own time, attend_forward(): lax.map(one_item, jnp.arange(head_count * block_count, dtype=jnp.int32))  31.5 us
  transfers between devices with their start and end apart: 19, of which 18 were waited for; matrix products, arithmetic and copies ran while one was open for 6% of the time, Pallas kernels for 0%

profile of v1, /device:TPU:0, one launch (start us, length us, event | category | flops | bytes accessed | tf_op | source)
XLA Modules:
  0.0 1007.0 jit_solution(9691578149097252202)
XLA Ops:
  9.1 10.3 %all-gather = bf16[8,1,128]{2,1,0:T(2,128)(2,1)S(1)} all-gather(bf16[1,1,128]{2,1,0:T(2,128)(2,1)} %bitcast.332), channel_id=1, replica_groups=mesh['dp'=8,'tensor'=4] {'dp'}, dimensions={0}, use_global_device_ids=true | all-gather | bytes 2304 | tf_op jit(solution)/shard_map/all_gather | solution.py:230
  21.9 2.1 fusion.77
  24.8 12.0 %all_gather.27 = bf16[256,1024]{1,0:T(8,128)(2,1)} all-gather(bf16[256,128]{1,0:T(8,128)(2,1)S(1)} %copy-done.24), channel_id=1, replica_groups=mesh['dp'=8,'tensor'=4] {'dp'}, dimensions={1}, use_global_device_ids=true | all-gather | bytes 589824 | tf_op jit(solution)/shard_map/all_gather | solution.py:232
  39.8 48.1 %all-gather.8.cloned.1.call-done = bf16[1024,1024]{1,0:T(8,128)(2,1)} async-done(((bf16[256,1024]{1,0:T(8,128)(2,1)}), bf16[1024,1024]{1,0:T(8,128)(2,1)}) %all-gather.8.cloned.1.call-update) | async-done | bytes 2097168 | tf_op jit(solution)/shard_map/all_gather | solution.py:189
  87.9 3.9 fusion.64
  96.9 70.2 %while.32 = (s32[]{:T(128)}, bf16[8,512,64]{1,2,0:T(8,128)(2,1)}, f32[8,512]{1,0:T(8,128)S(1)}, s32[8]{0:T(128)S(1)}, s32[2,512]{1,0:T(2,128)S(1)}, /*index=5*/s...) while((s32[]{:T(128)}, bf16[8,512,64]{1,2,0:T(8,128)(2,1)}, ...), condition=%wide.region_9.10_spmd.clone, body=%wide.region_6.9_spmd.sunk.clone | while | flops 138935840 | bytes 7109525 | solution.py:116
  103.5 2.2 fusion.153
  112.2 2.2 fusion.153
  121.0 2.2 fusion.153
  129.8 2.2 fusion.153
  138.5 2.2 fusion.153
  147.3 2.2 fusion.153
  156.1 2.2 fusion.153
  164.8 2.2 fusion.153
  169.1 3.7 fusion.95
  174.0 8.7 all-gather.1
  182.8 65.7 %reduce-scatter.9.cloned.1.call-done = f32[256,1024]{1,0:T(8,128)} async-done(((f32[1024,1024]{1,0:T(8,128)}), f32[256,1024]{1,0:T(8,128)}) %reduce-scatter.9.cloned.1.call-update) | async-done | bytes 1048592 | tf_op jit(solution)/shard_map/reduce_scatter | solution.py:201
  252.8 14.0 %collective-permute-done = bf16[256,1024]{1,0:T(8,128)(2,1)S(1)} collective-permute-done((bf16[256,1024]{1,0:T(8,128)(2,1)S(1)}, bf16[256,1024]{1,0:T(8,128)(2,1)S(1)}, u32[]{:S(2)}, u32[]{:S(2)}) %collective-permute-start) | collective-permute-done | bytes 524320 | tf_op jit(solution)/shard_map/ppermute | solution.py:22
  266.8 14.7 %collective-permute-done.1 = bf16[256,1024]{1,0:T(8,128)(2,1)} collective-permute-done((bf16[256,1024]{1,0:T(8,128)(2,1)S(1)}, bf16[256,1024]{1,0:T(8,128)(2,1)}, u32[]{:S(2)}, u32[]{:S(2)}) %collective-permute-start.1) | collective-permute-done | bytes 524320 | tf_op jit(solution)/shard_map/ppermute | solution.py:22
  287.2 8.8 collective-permute-done.2
  297.8 5.1 fusion.97
  302.9 5.5 all-gather.14.cloned.1.call-done
  308.5 48.0 %all-gather.12.cloned.1.call-done = bf16[1024,1024]{1,0:T(8,128)(2,1)} async-done(((bf16[256,1024]{1,0:T(8,128)(2,1)}), bf16[1024,1024]{1,0:T(8,128)(2,1)}) %all-gather.12.cloned.1.call-update) | async-done | bytes 2097168 | tf_op jit(solution)/shard_map/all_gather | solution.py:189
  356.5 5.5 fusion.60
  362.0 6.5 fusion.74
  371.1 5.0 convolution_bitcast_fusion.2
  376.2 5.3 fusion.96
  381.6 70.2 %reduce-scatter.13.cloned.1.call-done = f32[256,1024]{1,0:T(8,128)} async-done(((f32[1024,1024]{1,0:T(8,128)}), f32[256,1024]{1,0:T(8,128)}) %reduce-scatter.13.cloned.1.call-update) | async-done | bytes 1048592 | tf_op jit(solution)/shard_map/reduce_scatter | solution.py:214
  453.4 77.9 %reduce-scatter.11.cloned.1.call-done = f32[256,1024]{1,0:T(8,128)} async-done(((f32[1024,1024]{1,0:T(8,128)}), f32[256,1024]{1,0:T(8,128)}) %reduce-scatter.11.cloned.1.call-update) | async-done | bytes 1048592 | tf_op jit(solution)/shard_map/reduce_scatter | solution.py:201
  531.4 2.4 fusion.90
  536.5 14.0 %collective-permute-done.3 = bf16[256,1024]{1,0:T(8,128)(2,1)S(1)} collective-permute-done((bf16[256,1024]{1,0:T(8,128)(2,1)S(1)}, bf16[256,1024]{1,0:T(8,128)(2,1)S(1)}, u32[]{:S(2)}, u32[]{:S(2)}) %collective-permute-start.3) | collective-permute-done | bytes 524320 | tf_op jit(solution)/shard_map/ppermute | solution.py:22
  551.3 14.7 %collective-permute-done.4 = bf16[256,1024]{1,0:T(8,128)(2,1)} collective-permute-done((bf16[256,1024]{1,0:T(8,128)(2,1)S(1)}, bf16[256,1024]{1,0:T(8,128)(2,1)}, u32[]{:S(2)}, u32[]{:S(2)}) %collective-permute-start.4) | collective-permute-done | bytes 524320 | tf_op jit(solution)/shard_map/ppermute | solution.py:22
  568.5 11.8 %collective-permute-done.5 = bf16[256,1024]{1,0:T(8,128)(2,1)} collective-permute-done((bf16[256,1024]{1,0:T(8,128)(2,1)}, bf16[256,1024]{1,0:T(8,128)(2,1)}, u32[]{:S(2)}, u32[]{:S(2)}) %collective-permute-start.5) | collective-permute-done | bytes 524320 | tf_op jit(solution)/shard_map/ppermute | solution.py:22
  589.9 122.8 %while.33 = (s32[]{:T(128)}, f32[4,1024,64]{1,2,0:T(8,128)}, f32[4,1024,64]{1,2,0:T(8,128)}, f32[8,512,64]{1,2,0:T(8,128)}, s32[8]{0:T(128)S(1)}, /*index=5*/s32...) while((s32[]{:T(128)}, f32[4,1024,64]{1,2,0:T(8,128)}, ...), condition=%wide.region_19.20_spmd.clone, body=%wide.region_17.19_spmd.sunk.clone | while | flops 341016096 | bytes 19289032 | solution.py:178
  677.9 2.1 fusion.165
  712.7 3.1 copy.98
  715.8 2.1 reshape.229
  720.4 5.1 fusion.66
  725.5 5.2 convolution_bitcast_fusion.1
  732.2 4.8 fusion.99
  738.4 7.3 fusion.58
  750.2 19.8 %reduce-scatter.17.cloned.1.call-done = f32[3,128,256]{1,2,0:T(8,128)} async-done(((f32[3,1024,256]{1,2,0:T(8,128)}), f32[3,128,256]{1,2,0:T(8,128)}) %reduce-scatter.17.cloned.1.call-update) | async-done | bytes 393232 | tf_op jit(solution)/shard_map/reduce_scatter | solution.py:295
  771.9 77.0 %reduce-scatter.15.cloned.1.call-done = f32[256,1024]{1,0:T(8,128)} async-done(((f32[1024,1024]{1,0:T(8,128)}), f32[256,1024]{1,0:T(8,128)}) %reduce-scatter.15.cloned.1.call-update) | async-done | bytes 1048592 | tf_op jit(solution)/shard_map/reduce_scatter | solution.py:214
  852.4 13.9 %all-reduce.6 = (f32[1024]{0:T(1024)S(1)}, f32[1024]{0:T(1024)S(1)}) all-reduce(f32[1024]{0:T(1024)S(1)} %get-tuple-element.431, f32[1024]{0:T(1024)S(1)} %get-tuple-element.429), channel_id=6, replica_groups=mesh['dp'=8,'tensor'=4] {'dp'}, use_global_device_ids=true, to_apply=%region_25.26.clone | all-reduce | flops 2048 | bytes 16384
  866.5 11.7 %all-reduce.7 = (f32[128]{0:T(128)}, f32[128]{0:T(128)}) all-reduce(f32[128]{0:T(128)S(1)} %dynamic-slice.1, f32[128]{0:T(128)S(1)} %dynamic-slice.3), channel_id=1, replica_groups=mesh['dp'=8,'tensor'=4] {'tensor'}, use_global_device_ids=true, to_apply=%region_24.25 | all-reduce | flops 256 | bytes 2048 | tf_op jit(solution)/shard_map/psum | solution.py:292
  879.6 19.0 %reduce-scatter.23.cloned.1.call-done = f32[656,128]{1,0:T(8,128)} async-done(((f32[656,1024]{1,0:T(8,128)}), f32[656,128]{1,0:T(8,128)}) %reduce-scatter.23.cloned.1.call-update) | async-done | bytes 335888 | tf_op jit(solution)/shard_map/reduce_scatter | solution.py:299
  898.6 61.5 %reduce-scatter.21.cloned.1.call-done = f32[128,2,656]{0,2,1:T(8,128)} async-done(((f32[1024,2,656]{0,2,1:T(8,128)}), f32[128,2,656]{0,2,1:T(8,128)}) %reduce-scatter.21.cloned.1.call-update) | async-done | bytes 671760 | tf_op jit(solution)/shard_map/reduce_scatter | solution.py:298
  960.1 40.2 %reduce-scatter.19.cloned.1.call-done = f32[256,128]{1,0:T(8,128)} async-done(((f32[256,1024]{1,0:T(8,128)}), f32[256,128]{1,0:T(8,128)}) %reduce-scatter.19.cloned.1.call-update) | async-done | bytes 131088 | tf_op jit(solution)/shard_map/reduce_scatter | solution.py:296
  (294 shorter events, 174.1 us)
Async XLA Ops:
  7.2 17.0 %copy-start.27 = (s32[32]{0:T(128)S(1)}, s32[32]{0:T(128)}, u32[]{:S(2)}) copy-start(s32[32]{0:T(128)} %param.16) | copy-start | bytes 388
  7.2 17.1 %copy-start.28 = (s32[32]{0:T(128)S(1)}, s32[32]{0:T(128)}, u32[]{:S(2)}) copy-start(s32[32]{0:T(128)} %param.15) | copy-start | bytes 388
  7.2 17.6 %copy-start.24 = (bf16[256,128]{1,0:T(8,128)(2,1)S(1)}, bf16[256,128]{1,0:T(8,128)(2,1)}, u32[]{:S(2)}) copy-start(bf16[256,128]{1,0:T(8,128)(2,1)} %param.19) | copy-start | bytes 196612
  7.2 32.6 %all-gather.10.cloned.1.call-start = ((), (), s32[]{:S(2)}) async-start(), calls=%async_computation.9 | async-start | bytes 1769472 | tf_op jit(solution)/shard_map/all_gather | solution.py:231
  9.0 78.9 %all-gather.8.cloned.1.call-start = ((), (), s32[]{:S(2)}) async-start(), calls=%async_computation.8 | async-start | bytes 2621440 | tf_op jit(solution)/shard_map/all_gather | solution.py:189
  24.1 224.3 %reduce-scatter.9.cloned.1.call-start = ((), (), s32[]{:S(2)}) async-start(), calls=%async_computation.10 | async-start | bytes 5242880 | tf_op jit(solution)/shard_map/reduce_scatter | solution.py:201
  38.2 53.9 %copy-start.19 = (f32[1024,32]{0,1:T(8,128)}, f32[1024,32]{0,1:T(8,128)S(1)}, u32[]{:S(2)}) copy-start(f32[1024,32]{0,1:T(8,128)S(1)} %get-tuple-element.512) | copy-start | bytes 393220
  38.2 53.9 %copy-start.21 = (f32[1024,32]{0,1:T(8,128)}, f32[1024,32]{0,1:T(8,128)S(1)}, u32[]{:S(2)}) copy-start(f32[1024,32]{0,1:T(8,128)S(1)} %get-tuple-element.513) | copy-start | bytes 393220
  167.0 1.9 copy-start.8
  172.8 1.2 copy-start.25
  172.8 75.7 %copy-start = (bf16[256,1024]{1,0:T(8,128)(2,1)S(1)}, bf16[256,1024]{1,0:T(8,128)(2,1)}, u32[]{:S(2)}) copy-start(bf16[256,1024]{1,0:T(8,128)(2,1)} %param.14) | copy-start | bytes 1572868
  172.8 125.0 %all-gather.16.cloned.1.call-start = ((), (), s32[]{:S(2)}) async-start(), calls=%async_computation.13 | async-start | bytes 1511424 | tf_op jit(solution)/shard_map/all_gather | solution.py:235
  173.4 135.1 %all-gather.14.cloned.1.call-start = ((), (), s32[]{:S(2)}) async-start(), calls=%async_computation.12 | async-start | bytes 3022848 | tf_op jit(solution)/shard_map/all_gather | solution.py:234
  174.0 182.5 %all-gather.12.cloned.1.call-start = ((), (), s32[]{:S(2)}) async-start(), calls=%async_computation.11 | async-start | bytes 2621440 | tf_op jit(solution)/shard_map/all_gather | solution.py:189
  182.8 68.5 %copy-start.9 = (bf16[256,1024]{1,0:T(8,128)(2,1)S(1)}, bf16[256,1024]{1,0:T(8,128)(2,1)}, u32[]{:S(2)}) copy-start(bf16[256,1024]{1,0:T(8,128)(2,1)} %param.23) | copy-start | bytes 1572868
  251.2 200.6 %reduce-scatter.13.cloned.1.call-start = ((), (), s32[]{:S(2)}) async-start(), calls=%async_computation.15 | async-start | bytes 5242880 | tf_op jit(solution)/shard_map/reduce_scatter | solution.py:214
  251.2 15.5 %collective-permute-start = (bf16[256,1024]{1,0:T(8,128)(2,1)S(1)}, bf16[256,1024]{1,0:T(8,128)(2,1)S(1)}, u32[]{:S(2)}, u32[]{:S(2)}) collective-permute-start(bf16[256,1024]{1,0:T(8,128)(2,1)S(1)} %copy-done.9), channel_id=1, source_target_pairs={{0,1},{1,2},{2,3},{3,0},{4,5},{5,6},{6,7},{7,4},{8,9},{9,10},{10,1... | collective-permute-start | bytes 1572872 | tf_op jit(solution)/shard_map/ppermute | solution.py:22
  266.8 14.7 %collective-permute-start.1 = (bf16[256,1024]{1,0:T(8,128)(2,1)S(1)}, bf16[256,1024]{1,0:T(8,128)(2,1)}, u32[]{:S(2)}, u32[]{:S(2)}) collective-permute-start(bf16[256,1024]{1,0:T(8,128)(2,1)S(1)} %collective-permute-done), channel_id=1, source_target_pairs={{0,1},{1,2},{2,3},{3,0},{4,5},{5,6},{6,7},{7,4},{8,9},{9,10},{10,1... | collective-permute-start | bytes 1572872 | tf_op jit(solution)/shard_map/ppermute | solution.py:22
  281.5 14.5 %collective-permute-start.2 = (bf16[256,1024]{1,0:T(8,128)(2,1)}, bf16[256,1024]{1,0:T(8,128)(2,1)}, u32[]{:S(2)}, u32[]{:S(2)}) collective-permute-start(bf16[256,1024]{1,0:T(8,128)(2,1)} %collective-permute-done.1), channel_id=1, source_target_pairs={{0,1},{1,2},{2,3},{3,0},{4,5},{5,6},{6,7},{7,4},{8,9},{9,10},{10,1... | collective-permute-start | bytes 1572872 | tf_op jit(solution)/shard_map/ppermute | solution.py:22
  356.5 5.5 copy-start.2
  368.5 1.6 copy-start.14
  368.5 2.6 copy-start.26
  370.0 1.1 copy-start.16
  370.0 6.1 copy-start.17
  376.1 155.2 %reduce-scatter.11.cloned.1.call-start = ((), (), s32[]{:S(2)}) async-start(), calls=%async_computation.14 | async-start | bytes 5242880 | tf_op jit(solution)/shard_map/reduce_scatter | solution.py:201
  381.5 388.5 %reduce-scatter.17.cloned.1.call-start = ((), (), s32[]{:S(2)}) async-start(), calls=%async_computation.17 | async-start | bytes 3538944 | tf_op jit(solution)/shard_map/reduce_scatter | solution.py:295
  451.7 79.6 %copy-start.12 = (f32[256,1024]{1,0:T(8,128)S(1)}, f32[256,1024]{1,0:T(8,128)}, u32[]{:S(2)}) copy-start(f32[256,1024]{1,0:T(8,128)} %reduce-scatter.13.cloned.1.call-done) | copy-start | bytes 3145732
  531.4 3.4 copy-start.10
  533.8 1.0 copy-start.4
  535.0 15.5 %collective-permute-start.3 = (bf16[256,1024]{1,0:T(8,128)(2,1)S(1)}, bf16[256,1024]{1,0:T(8,128)(2,1)S(1)}, u32[]{:S(2)}, u32[]{:S(2)}) collective-permute-start(bf16[256,1024]{1,0:T(8,128)(2,1)S(1)} %get-tuple-element.482), channel_id=1, source_target_pairs={{0,1},{1,2},{2,3},{3,0},{4,5},{5,6},{6,7},{7,4},{8,9},{9,10},{10,1... | collective-permute-start | bytes 1572872 | tf_op jit(solution)/shard_map/ppermute | solution.py:22
  551.3 14.7 %collective-permute-start.4 = (bf16[256,1024]{1,0:T(8,128)(2,1)S(1)}, bf16[256,1024]{1,0:T(8,128)(2,1)}, u32[]{:S(2)}, u32[]{:S(2)}) collective-permute-start(bf16[256,1024]{1,0:T(8,128)(2,1)S(1)} %collective-permute-done.3), channel_id=1, source_target_pairs={{0,1},{1,2},{2,3},{3,0},{4,5},{5,6},{6,7},{7,4},{8,9},{9,10},{10,1... | collective-permute-start | bytes 1572872 | tf_op jit(solution)/shard_map/ppermute | solution.py:22
  566.1 14.2 %collective-permute-start.5 = (bf16[256,1024]{1,0:T(8,128)(2,1)}, bf16[256,1024]{1,0:T(8,128)(2,1)}, u32[]{:S(2)}, u32[]{:S(2)}) collective-permute-start(bf16[256,1024]{1,0:T(8,128)(2,1)} %collective-permute-done.4), channel_id=1, source_target_pairs={{0,1},{1,2},{2,3},{3,0},{4,5},{5,6},{6,7},{7,4},{8,9},{9,10},{10,1... | collective-permute-start | bytes 1572872 | tf_op jit(solution)/shard_map/ppermute | solution.py:22
  566.2 15.1 %copy-start.13 = (bf16[256,1024]{1,0:T(8,128)(2,1)S(1)}, bf16[256,1024]{1,0:T(8,128)(2,1)}, u32[]{:S(2)}) copy-start(bf16[256,1024]{1,0:T(8,128)(2,1)} %all_gather.27) | copy-start | bytes 1572868
  581.3 1.6 copy-start.6
  712.7 5.2 copy-start.1
  712.7 5.2 copy-start.20
  712.7 5.3 copy-start.22
  725.5 123.5 %reduce-scatter.15.cloned.1.call-start = ((), (), s32[]{:S(2)}) async-start(), calls=%async_computation.16 | async-start | bytes 5242880 | tf_op jit(solution)/shard_map/reduce_scatter | solution.py:214
  730.8 1.4 copy-start.18
  730.8 167.8 %reduce-scatter.23.cloned.1.call-start = ((), (), s32[]{:S(2)}) async-start(), calls=%async_computation.20 | async-start | bytes 3022848 | tf_op jit(solution)/shard_map/reduce_scatter | solution.py:299
  737.0 1.4 copy-start.15
  737.0 223.0 %reduce-scatter.21.cloned.1.call-start = ((), (), s32[]{:S(2)}) async-start(), calls=%async_computation.19 | async-start | bytes 6045696 | tf_op jit(solution)/shard_map/reduce_scatter | solution.py:298
  745.6 1.6 copy-start.7
  745.7 3.3 copy-start.29
  745.7 254.6 %reduce-scatter.19.cloned.1.call-start = ((), (), s32[]{:S(2)}) async-start(), calls=%async_computation.18 | async-start | bytes 1179648 | tf_op jit(solution)/shard_map/reduce_scatter | solution.py:296
  748.9 129.2 %copy-start.5 = (f32[256,1024]{1,0:T(8,128)S(1)}, f32[256,1024]{1,0:T(8,128)}, u32[]{:S(2)}) copy-start(f32[256,1024]{1,0:T(8,128)} %copy-done.4) | copy-start | bytes 3145732
  748.9 129.2 %copy-start.11 = (bf16[256,1024]{1,0:T(8,128)(2,1)S(1)}, bf16[256,1024]{1,0:T(8,128)(2,1)}, u32[]{:S(2)}) copy-start(bf16[256,1024]{1,0:T(8,128)(2,1)} %param.23) | copy-start | bytes 1572868
  849.0 29.2 %copy-start.3 = (f32[256,1024]{1,0:T(8,128)S(1)}, f32[256,1024]{1,0:T(8,128)}, u32[]{:S(2)}) copy-start(f32[256,1024]{1,0:T(8,128)} %reduce-scatter.15.cloned.1.call-done) | copy-start | bytes 3145732
  (1 other events, 0.8 us)
Sparse Core Ops, SparseCore 0:
  10.5 29.2 all-gather.9
  42.0 45.9 all-gather.7
  172.9 75.4 reduce-scatter.8
  250.3 25.3 all-gather.15
  277.6 30.7 all-gather.13
  310.5 45.9 all-gather.11
  376.2 75.4 reduce-scatter.12
  454.0 77.2 reduce-scatter.10
  725.6 44.3 reduce-scatter.16
  772.2 76.7 reduce-scatter.14
  853.4 45.1 reduce-scatter.22
  902.8 57.1 reduce-scatter.20
  964.1 36.0 reduce-scatter.18
